TPU v7x, 512 devices: a whole 4x8x8 slice. The times are simulated.
512 devices in a mesh: pool: 32 (over z_hi, y), ctx: 4 (over x), head: 4 (over z_lo, core).
Axes of the slice: x: 4, y: 8, z: 8 (z_hi: 4, z_lo: 2; z = z_hi * 2 + z_lo), core: 2. Of those that a mesh axis runs over, the one named last changes fastest.
Arguments:
- kv_pool: bfloat16 [4, 1024, 2, 32, 1024], P('ctx', 'pool', None, None, 'head'), may hold values from -6 to 6
- state_pool: bfloat16 [1024, 64, 1024], P('pool', 'ctx', 'head'), may hold values from -0.59765625 to 0.59765625
- block_owner: int32 [4, 1024], P('ctx'), may hold values from 0 to 31, as said below
- block_index: int32 [4, 1024], P('ctx'), may hold values from 0 to 31, as said below
- history_len: int32 [32], P('pool'), may hold values from 1 to 4096, as said below
- turn_len: int32 [32], P('pool'), may hold values from 256 to 512, as said below
- mixer_in: bfloat16 [32, 128, 64, 512], P('pool', 'head', 'ctx'), may hold values from -6 to 6
- input_proj: bfloat16 [32, 8, 256, 512], P('pool', 'head'), may hold values from -1.5 to 1.5
- output_proj: bfloat16 [32, 8, 256, 512], P('pool', 'head'), may hold values from -6 to 6
- step_size: float32 [32, 128, 512], P('pool', 'head'), may hold values from 0 to 2, as said below
- decay_rate: float32 [128], P('head'), may hold values from 0 to 4, as said below
- bypass_factor: float32 [128], P('head'), may hold values from 0.5 to 1.5
- queries: bfloat16 [32, 512, 8192], P('pool', 'ctx', 'head'), may hold values from -300 to 300
- turn_kv: bfloat16 [32, 2, 512, 1024], P('pool', None, 'ctx', 'head'), may hold values from -6 to 6
Outputs:
- mixer_out: bfloat16 [32, 128, 64, 512], P('pool', 'head', 'ctx')
- next_state: float32 [32, 128, 64, 256], P('pool', 'head', 'ctx')
- attn_out: bfloat16 [32, 512, 8192], P('pool', 'ctx', 'head')
Inputs may be any that keep to these rules, and one draw needn't show every extreme that they name: `block_owner`: in each row c, every session owns exactly 32 slots, and each aligned run of 32 slots (one pool shard) holds at most 2 blocks of any one session; in every row some shard holds exactly 2 blocks of some session. `block_index`: in each row, the slots of one session carry the indices 0 to 31, each once. `history_len`: some session has exactly 4096. `turn_len`: every value is at least 256 and some session has exactly 512. `step_size`: Positive. `decay_rate`: Positive.
All inputs are finite; a program needn't handle non-finite values.
Results may differ from a plain program's by a relative error of at most 0.008.
Values may be sent and summed in bfloat16 or wider, within the bound.
A program may use at most 64 MiB of HBM per device.

v0:
```python
import jax
import jax.numpy as jnp
from jax import lax
from jax.sharding import PartitionSpec as P

Q_HEADS = 64
KV_HEADS = 8
HEAD_DIM = 128
PAGE = 32
BLK = 128


floor_score = -1e30


def spanned_ssd(
    values, input_proj, output_proj, step_sizes, rates, bypass_factor, start_state, valid_len
):
    heads, channels, total = values.shape
    groups = input_proj.shape[0]
    per_group = heads // groups
    count = total // BLK
    positions = jnp.arange(total, dtype=jnp.int32)
    live = positions < valid_len
    step_sizes = jnp.where(live[None, :], step_sizes, jnp.float32(0.0))
    value_blocks = values.reshape(heads, channels, count, BLK).transpose(2, 0, 1, 3)
    input_blocks = input_proj.reshape(groups, -1, count, BLK).transpose(2, 0, 1, 3)
    output_blocks = output_proj.reshape(groups, -1, count, BLK).transpose(2, 0, 1, 3)
    step_blocks = step_sizes.reshape(heads, count, BLK).transpose(1, 0, 2)
    offsets = jnp.arange(BLK, dtype=jnp.int32)
    lower = offsets[:, None] >= offsets[None, :]
    exact = lax.Precision.HIGHEST

    def advance(carried, item):
        value_blk, input_blk, output_blk, step_blk = item
        value_blk = value_blk.astype(jnp.float32)
        input_blk = input_blk.astype(jnp.float32)
        output_blk = output_blk.astype(jnp.float32)
        running = jnp.cumsum(-rates[:, None] * step_blk, axis=1)
        pairs = jnp.einsum("gnt,gns->gts", output_blk, input_blk, precision=exact)
        pairs = jnp.repeat(pairs, per_group, axis=0)
        gaps = jnp.minimum(running[:, :, None] - running[:, None, :], 0.0)
        mixing = jnp.where(lower[None], jnp.exp(gaps), 0.0) * pairs * step_blk[:, None, :]
        result = jnp.einsum("hts,hps->hpt", mixing, value_blk, precision=exact)
        read_out = jnp.repeat(output_blk, per_group, axis=0)
        result = result + jnp.exp(running)[:, None, :] * jnp.einsum(
            "hpn,hnt->hpt", carried, read_out, precision=exact
        )
        result = result + bypass_factor[:, None, None] * value_blk
        weights = jnp.exp(running[:, -1:] - running) * step_blk
        write_in = jnp.repeat(input_blk, per_group, axis=0)
        carried = jnp.exp(running[:, -1])[:, None, None] * carried + jnp.einsum(
            "hps,hns->hpn", value_blk * weights[:, None, :], write_in, precision=exact
        )
        return (carried, result)

    final_state, results = lax.scan(
        advance, start_state, (value_blocks, input_blocks, output_blocks, step_blocks)
    )
    results = results.transpose(1, 2, 0, 3).reshape(heads, channels, total)
    return (jnp.where(live[None, None, :], results, 0.0), final_state)


def route_blocks(kv_local, state_local, owner_row, index_row):
    parties = lax.axis_size("pool")
    myself = lax.axis_index("pool")
    pages = kv_local.shape[1]
    capacity = 2 * pages // parties
    sessions = jnp.arange(parties, dtype=jnp.int32)
    table = (
        (owner_row[:, None] == sessions[None, :]).astype(jnp.int32).reshape(parties, pages, parties)
    )
    before = jnp.cumsum(table, axis=1) - table
    ranks = jnp.sum(before * table, axis=2)
    owners = owner_row.reshape(parties, pages)
    my_owner = lax.dynamic_index_in_dim(owners, myself, 0, keepdims=False)
    device_rank = lax.dynamic_index_in_dim(ranks, myself, 0, keepdims=False)
    send_kv = (
        jnp.zeros((parties, capacity) + kv_local.shape[2:], kv_local.dtype)
        .at[my_owner, device_rank]
        .set(kv_local[0])
    )
    send_state = (
        jnp.zeros((parties, capacity) + state_local.shape[1:], state_local.dtype)
        .at[my_owner, device_rank]
        .set(state_local)
    )
    recv_kv, recv_state = (
        lax.all_to_all(send_kv, "pool", split_axis=0, concat_axis=0, tiled=True),
        lax.all_to_all(send_state, "pool", split_axis=0, concat_axis=0, tiled=True),
    )
    flat_place = (sessions[:, None] * capacity + ranks).reshape(-1)
    target = jnp.where(owner_row == myself, index_row, pages)
    where_from = jnp.zeros((pages,), jnp.int32).at[target].set(flat_place, mode="drop")
    hist_pages = recv_kv.reshape((parties * capacity,) + recv_kv.shape[2:])[where_from]
    start_slabs = recv_state.reshape((parties * capacity,) + recv_state.shape[2:])[where_from]
    return (hist_pages, start_slabs)


def attend_block(carried, query_rows, query_index, block, seg_id, hist_rows, history_len):
    rows = query_rows.shape[0]
    key_rows = block.shape[1]
    width = block.shape[2]
    groups = width // HEAD_DIM
    per_group = Q_HEADS // KV_HEADS
    turn_rows = key_rows - hist_rows
    offsets = jnp.arange(key_rows, dtype=jnp.int32)
    in_history = offsets < hist_rows
    placed = jnp.where(
        in_history, seg_id * hist_rows + offsets, seg_id * turn_rows + offsets - hist_rows
    )
    seen_mask = jnp.where(
        in_history[None, :],
        (placed < history_len)[None, :],
        placed[None, :] <= query_index[:, None],
    )
    score_scale = HEAD_DIM ** (-0.5)
    peak, totals, summed = carried
    query_heads = query_rows.reshape(rows, groups, per_group, HEAD_DIM)
    key_heads = block[0].reshape(key_rows, groups, HEAD_DIM)
    value_heads = block[1].reshape(key_rows, groups, HEAD_DIM)
    scores = (
        jnp.einsum("rgqd,kgd->rgqk", query_heads, key_heads, preferred_element_type=jnp.float32)
        * score_scale
    )
    mask = seen_mask[:, None, None, :]
    fresh = jnp.maximum(peak, jnp.max(jnp.where(mask, scores, floor_score), axis=-1))
    weights = jnp.where(mask, jnp.exp(scores - fresh[..., None]), 0.0)
    fade = jnp.exp(peak - fresh)
    totals = fade * totals + jnp.sum(weights, axis=-1)
    summed = fade[..., None] * summed + jnp.einsum(
        "rgqk,kgd->rgqd",
        weights.astype(jnp.bfloat16),
        value_heads,
        preferred_element_type=jnp.float32,
    )
    return (fresh, totals, summed)


def context_attention(query_rows, history, turn_keys, history_len, turn_len):
    turn_rows = query_rows.shape[0]
    hist_rows = history.shape[1]
    seg_rows = hist_rows + turn_rows
    width = history.shape[-1]
    groups = width // HEAD_DIM
    per_group = Q_HEADS // KV_HEADS
    segment = lax.axis_index("ctx")
    local_keys = jnp.concatenate([history, turn_keys], axis=1)
    row_ids = jnp.arange(turn_rows, dtype=jnp.int32)
    own_index = segment * turn_rows + row_ids
    carried = (
        jnp.full((turn_rows, groups, per_group), floor_score, jnp.float32),
        jnp.zeros((turn_rows, groups, per_group), jnp.float32),
        jnp.zeros((turn_rows, groups, per_group, HEAD_DIM), jnp.float32),
    )
    piece = lax.all_gather(local_keys, "ctx", axis=1, tiled=True)
    count = piece.shape[1] // seg_rows
    blocks = piece.reshape(2, count, seg_rows, width).transpose(1, 0, 2, 3)

    def visit(inner, item):
        block, offset = item
        return (
            attend_block(inner, query_rows, own_index, block, offset, hist_rows, history_len),
            None,
        )

    carried, _ = lax.scan(visit, carried, (blocks, jnp.arange(count, dtype=jnp.int32)))
    peak, totals, summed = carried
    result = (summed / totals[..., None]).reshape(turn_rows, groups * per_group * HEAD_DIM)
    return jnp.where((own_index < turn_len)[:, None], result, 0.0).astype(jnp.bfloat16)


def local(
    kv_pool,
    state_pool,
    block_owner,
    block_index,
    history_len,
    turn_len,
    mixer_in,
    input_proj,
    output_proj,
    step_size,
    decay_rate,
    bypass_factor,
    queries,
    turn_kv,
):
    hist_pages, start_slabs = route_blocks(kv_pool, state_pool, block_owner[0], block_index[0])
    pages = hist_pages.shape[0]
    width = hist_pages.shape[-1]
    history = hist_pages.transpose(1, 0, 2, 3).reshape(2, pages * PAGE, width)
    mixed, final = spanned_ssd(
        mixer_in[0],
        input_proj[0],
        output_proj[0],
        step_size[0],
        decay_rate,
        bypass_factor,
        start_slabs.astype(jnp.float32),
        turn_len[0],
    )
    attended = context_attention(queries[0], history, turn_kv[0], history_len[0], turn_len[0])
    return (mixed.astype(jnp.bfloat16)[None], final[None], attended[None])


def solution(mesh):
    return jax.shard_map(
        local,
        mesh=mesh,
        in_specs=(
            P("ctx", "pool", None, None, "head"),
            P("pool", "ctx", "head"),
            P("ctx", None),
            P("ctx", None),
            P("pool"),
            P("pool"),
            P("pool", "head", "ctx", None),
            P("pool", "head", None, None),
            P("pool", "head", None, None),
            P("pool", "head", None),
            P("head"),
            P("head"),
            P("pool", "ctx", "head"),
            P("pool", None, "ctx", "head"),
        ),
        out_specs=(
            P("pool", "head", "ctx", None),
            P("pool", "head", "ctx", None),
            P("pool", "ctx", "head"),
        ),
        check_vma=False,
    )
```

profile of v0, /device:TPU:1, one launch (start us, length us, event | category | flops | bytes accessed | tf_op | source)
XLA Modules:
  0.0 286.1 jit_solution(10285035328454896795)
XLA Ops:
  7.7 1.3 reduce.7
  9.2 1.0 fusion.51
  10.4 0.9 broadcast_in_dim.176
  11.3 4.3 %scatter_fusion = bf16[32,2,16,256]{3,2,1,0:T(8,128)(2,1)} fusion(bf16[32,2,16,256]{3,2,1,0:T(8,128)(2,1)} %broadcast_in_dim.176, s32[32]{0:T(128)S(1)} %fusion.47, bf16[32,16,256]{2,1,0:T(8,128)(2,1)} %param.19), kind=kCustom, calls=%fused_computation.2 | custom fusion | bytes 786688 | tf_op jit(solution)/shard_map/scatter | solution.py:86
  15.6 16.5 %all-to-all-start = ((bf16[32,2,16,256]{3,2,1,0:T(8,128)(2,1)}), bf16[32,2,16,256]{3,2,1,0:T(8,128)(2,1)S(1)}, u32[]{:S(2)}, u32[]{:S(2)}) async-start(bf16[32,2,16,256]{3,2,1,0:T(8,128)(2,1)} %scatter_fusion), calls=%async_computation | async-start | bytes 1048576 | tf_op jit(solution)/shard_map/all_to_all | solution.py:90
  32.1 1.6 broadcast_in_dim.189
  33.7 5.1 %scatter_fusion.1 = bf16[32,2,2,32,256]{4,3,2,1,0:T(8,128)(2,1)} fusion(bf16[32,2,2,32,256]{4,3,2,1,0:T(8,128)(2,1)} %broadcast_in_dim.189, s32[32]{0:T(128)S(1)} %fusion.47, bf16[32,2,32,256]{3,2,1,0:T(8,128)(2,1)S(1)} %bitcast.210), kind=kCustom, calls=%fused_computation.4 | custom fusion | bytes 3145984 | tf_op jit(solution)/shard_map/scatter | solution.py:81
  38.8 9.6 %all-to-all-done = bf16[32,2,16,256]{3,2,1,0:T(8,128)(2,1)S(1)} async-done(((bf16[32,2,16,256]{3,2,1,0:T(8,128)(2,1)}), bf16[32,2,16,256]{3,2,1,0:T(8,128)(2,1)S(1)}, u32[]{:S(2)}, u32[]{:S(2)}) %all-to-all-start) | async-done | bytes 524320 | tf_op jit(solution)/shard_map/all_to_all | solution.py:90
  48.4 8.1 %all-to-all-start.1 = ((bf16[32,2,2,32,256]{4,3,2,1,0:T(8,128)(2,1)}), bf16[32,2,2,32,256]{4,3,2,1,0:T(8,128)(2,1)}, u32[]{:S(2)}, u32[]{:S(2)}) async-start(bf16[32,2,2,32,256]{4,3,2,1,0:T(8,128)(2,1)} %scatter_fusion.1), calls=%async_computation.1 | async-start | bytes 4194304 | tf_op jit(solution)/shard_map/all_to_all | solution.py:89
  58.2 4.5 %scatter_custom_fusion.1 = s32[32]{0:T(128)S(1)} fusion(s32[1024]{0:T(1024)S(1)} %bitcast.214, s32[1024]{0:T(1024)S(1)} %reshape.369, s32[]{:T(128)} %constant.117.clone.1), kind=kCustom, calls=%fused_computation.95 | custom fusion | bytes 132 | tf_op jit(solution)/shard_map/scatter | solution.py:94
  64.5 49.6 %all-to-all-done.1 = bf16[32,2,2,32,256]{4,3,2,1,0:T(8,128)(2,1)} async-done(((bf16[32,2,2,32,256]{4,3,2,1,0:T(8,128)(2,1)}), bf16[32,2,2,32,256]{4,3,2,1,0:T(8,128)(2,1)}, u32[]{:S(2)}, u32[]{:S(2)}) %all-to-all-start.1) | async-done | bytes 2097184 | tf_op jit(solution)/shard_map/all_to_all | solution.py:89
  114.1 3.2 %gather_fusion.1 = bf16[32,2,32,256]{3,2,1,0:T(8,128)(2,1)} fusion(bf16[64,2,32,256]{3,2,1,0:T(8,128)(2,1)} %bitcast.17, s32[1024]{0:T(1024)S(1)} %pad_clamp_fusion), kind=kCustom, calls=%fused_computation.1 | custom fusion | bytes 2097280 | tf_op jit(solution)/shard_map/gather | solution.py:95
  117.3 1.3 copy.80
  118.6 1.1 pad_maximum_fusion
  119.7 52.2 %while.32 = (s32[]{:T(128)}, f32[32,16,256]{2,1,0:T(8,128)S(1)}, bf16[4,32,16,128]{3,2,1,0:T(8,128)(2,1)}, f32[32,1]{0,1:T(1,128)S(1)}, f32[4,32,128]{2,0,1:T(4,...) while((s32[]{:T(128)}, f32[32,16,256]{2,1,0:T(8,128)S(1)}, ...), condition=%wide.region_6.7_spmd.clone, body=%wide.region_4.6_spmd.clone.sunk | while | flops 524115968 | bytes 31068848 | solution.py:57
  121.0 1.7 fusion.87
  124.6 3.1 %fusion.88 = bf16[4,32,16,128]{3,2,1,0:T(8,128)(2,1)S(1)} fusion(bf16[4,32,16,128]{3,2,1,0:T(8,128)(2,1)S(1)} %copy-done.8, s32[]{:T(128)} %get-tuple-element.550, f32[32,16,128]{2,1,0:T(8,128)S(1)} %fusion.87, f32[32,256,128]{2,1,0:T(8,128)S(1)} %bitcast.192, f32[32,16,256]{2,1,0:T(8,128)S(1)} %get-tuple-element.551, f32[32]{0:T(128)} %get-tuple-element.569, ...), kind=kOutput, calls=%fused_computation.42.clone.1 | convolution fusion | flops 201654272 | bytes 5390468 | tf_op jit(solution)/shard_map/while/body/eval_jaxpr/hpn,hnt->hpt/dot_general | solution.py:46
  127.7 0.8 copy-done.9
  129.2 3.6 %convolution_add_fusion.2 = f32[32,16,256]{2,1,0:T(8,128)S(1)} fusion(f32[32,256,128]{2,1,0:T(8,128)S(1)} %bitcast.193, f32[32,16,256]{2,1,0:T(8,128)S(1)} %get-tuple-element.551, f32[32]{0:T(128)S(1)} %exp.74, f32[32,128]{1,0:T(8,128)S(1)} %get-tuple-element.520, bf16[4,32,16,128]{3,2,1,0:T(8,128)(2,1)S(1)} %get-tuple-element.566, ...), kind=kOutput, calls=%fused_computation.36.clone.1 | convolution fusion | flops 201719808 | bytes 5390852 | tf_op jit(solution)/shard_map/while/body/eval_jaxpr/hps,hns->hpn/dot_general | solution.py:52
  134.0 1.7 fusion.87
  137.7 3.1 %fusion.88 = bf16[4,32,16,128]{3,2,1,0:T(8,128)(2,1)S(1)} fusion(bf16[4,32,16,128]{3,2,1,0:T(8,128)(2,1)S(1)} %copy-done.8, s32[]{:T(128)} %get-tuple-element.550, f32[32,16,128]{2,1,0:T(8,128)S(1)} %fusion.87, f32[32,256,128]{2,1,0:T(8,128)S(1)} %bitcast.192, f32[32,16,256]{2,1,0:T(8,128)S(1)} %get-tuple-element.551, f32[32]{0:T(128)} %get-tuple-element.569, ...), kind=kOutput, calls=%fused_computation.42.clone.1 | convolution fusion | flops 201654272 | bytes 5390468 | tf_op jit(solution)/shard_map/while/body/eval_jaxpr/hpn,hnt->hpt/dot_general | solution.py:46
  140.8 0.8 copy-done.9
  142.2 3.6 %convolution_add_fusion.2 = f32[32,16,256]{2,1,0:T(8,128)S(1)} fusion(f32[32,256,128]{2,1,0:T(8,128)S(1)} %bitcast.193, f32[32,16,256]{2,1,0:T(8,128)S(1)} %get-tuple-element.551, f32[32]{0:T(128)S(1)} %exp.74, f32[32,128]{1,0:T(8,128)S(1)} %get-tuple-element.520, bf16[4,32,16,128]{3,2,1,0:T(8,128)(2,1)S(1)} %get-tuple-element.566, ...), kind=kOutput, calls=%fused_computation.36.clone.1 | convolution fusion | flops 201719808 | bytes 5390852 | tf_op jit(solution)/shard_map/while/body/eval_jaxpr/hps,hns->hpn/dot_general | solution.py:52
  147.1 1.7 fusion.87
  150.7 3.1 %fusion.88 = bf16[4,32,16,128]{3,2,1,0:T(8,128)(2,1)S(1)} fusion(bf16[4,32,16,128]{3,2,1,0:T(8,128)(2,1)S(1)} %copy-done.8, s32[]{:T(128)} %get-tuple-element.550, f32[32,16,128]{2,1,0:T(8,128)S(1)} %fusion.87, f32[32,256,128]{2,1,0:T(8,128)S(1)} %bitcast.192, f32[32,16,256]{2,1,0:T(8,128)S(1)} %get-tuple-element.551, f32[32]{0:T(128)} %get-tuple-element.569, ...), kind=kOutput, calls=%fused_computation.42.clone.1 | convolution fusion | flops 201654272 | bytes 5390468 | tf_op jit(solution)/shard_map/while/body/eval_jaxpr/hpn,hnt->hpt/dot_general | solution.py:46
  153.8 0.8 copy-done.9
  155.2 3.6 %convolution_add_fusion.2 = f32[32,16,256]{2,1,0:T(8,128)S(1)} fusion(f32[32,256,128]{2,1,0:T(8,128)S(1)} %bitcast.193, f32[32,16,256]{2,1,0:T(8,128)S(1)} %get-tuple-element.551, f32[32]{0:T(128)S(1)} %exp.74, f32[32,128]{1,0:T(8,128)S(1)} %get-tuple-element.520, bf16[4,32,16,128]{3,2,1,0:T(8,128)(2,1)S(1)} %get-tuple-element.566, ...), kind=kOutput, calls=%fused_computation.36.clone.1 | convolution fusion | flops 201719808 | bytes 5390852 | tf_op jit(solution)/shard_map/while/body/eval_jaxpr/hps,hns->hpn/dot_general | solution.py:52
  160.1 1.7 fusion.87
  163.8 3.1 %fusion.88 = bf16[4,32,16,128]{3,2,1,0:T(8,128)(2,1)S(1)} fusion(bf16[4,32,16,128]{3,2,1,0:T(8,128)(2,1)S(1)} %copy-done.8, s32[]{:T(128)} %get-tuple-element.550, f32[32,16,128]{2,1,0:T(8,128)S(1)} %fusion.87, f32[32,256,128]{2,1,0:T(8,128)S(1)} %bitcast.192, f32[32,16,256]{2,1,0:T(8,128)S(1)} %get-tuple-element.551, f32[32]{0:T(128)} %get-tuple-element.569, ...), kind=kOutput, calls=%fused_computation.42.clone.1 | convolution fusion | flops 201654272 | bytes 5390468 | tf_op jit(solution)/shard_map/while/body/eval_jaxpr/hpn,hnt->hpt/dot_general | solution.py:46
  166.9 0.8 copy-done.9
  168.3 3.6 %convolution_add_fusion.2 = f32[32,16,256]{2,1,0:T(8,128)S(1)} fusion(f32[32,256,128]{2,1,0:T(8,128)S(1)} %bitcast.193, f32[32,16,256]{2,1,0:T(8,128)S(1)} %get-tuple-element.551, f32[32]{0:T(128)S(1)} %exp.74, f32[32,128]{1,0:T(8,128)S(1)} %get-tuple-element.520, bf16[4,32,16,128]{3,2,1,0:T(8,128)(2,1)S(1)} %get-tuple-element.566, ...), kind=kOutput, calls=%fused_computation.36.clone.1 | convolution fusion | flops 201719808 | bytes 5390852 | tf_op jit(solution)/shard_map/while/body/eval_jaxpr/hps,hns->hpn/dot_general | solution.py:52
  171.9 1.6 copy.79
  173.8 1.6 select_convert_fusion.1
  175.4 7.0 %all-gather.2.cloned.1.call-done = bf16[2,4608,256]{2,1,0:T(8,128)(2,1)} async-done(((bf16[2,1152,256]{2,1,0:T(8,128)(2,1)}), bf16[2,4608,256]{2,1,0:T(8,128)(2,1)}) %all-gather.2.cloned.1.call-update) | async-done | bytes 4718608 | tf_op jit(solution)/shard_map/all_gather | solution.py:156
  182.4 94.4 %while.33 = (s32[]{:T(128)}, f32[128,2,8]{0,2,1:T(8,128)S(1)}, f32[128,2,8]{0,2,1:T(8,128)S(1)}, f32[128,2,8,128]{0,3,2,1:T(8,128)}, s32[4]{0:T(128)S(1)}, /*ind...) while((s32[]{:T(128)}, f32[128,2,8]{0,2,1:T(8,128)S(1)}, ...), condition=%wide.region_11.12_spmd.clone, body=%wide.region_8.11_spmd.clone.sunk | while | flops 1235016192 | bytes 47004440 | solution.py:167
  184.5 0.7 iota_compare_fusion.8
  185.2 1.1 compare_select_fusion.7
  186.2 1.3 constant_dynamic-slice_fusion.10
  188.0 5.3 %fusion.92 = (f32[128,2,8]{0,2,1:T(8,128)S(1)}, f32[2,1152,128,8]{2,1,3,0:T(8,128)}) fusion(pred[128,1152]{0,1:T(8,128)(4,1)S(1)} %compare_select_fusion.7, bf16[1152,2,128,1]{0,2,3,1:T(8,128)(2,1)S(1)} %bitcast.196, bf16[128,2,8,128]{3,2,1,0:T(8,128)(2,1)S(1)} %bitcast.194), kind=kOutput, calls=%fused_computation.9.clone.1 | convolution fusion | flops 611055616 | bytes 10706944 | tf_op jit(solution)/shard_map/while/body/eval_jaxpr/rgqd,kgd->rgqk/dot_general | solution.py:123
  193.3 5.6 %fusion.93 = f32[128,2,8]{0,2,1:T(8,128)S(1)} fusion(f32[2,1152,128,8]{2,1,3,0:T(8,128)} %get-tuple-element.535, f32[128,2,8]{0,2,1:T(8,128)S(1)} %select_maximum_fusion.2, pred[128,1152]{0,1:T(8,128)(4,1)S(1)} %compare_select_fusion.7), kind=kLoop, calls=%fused_computation.13.clone.1 | loop fusion | flops 9435136 | bytes 9601024 | tf_op jit(solution)/shard_map/while/body/eval_jaxpr/reduce_sum | solution.py:130
  199.2 5.9 %fusion.95 = f32[128,2,8,128]{0,3,2,1:T(8,128)S(1)} fusion(bf16[1152,2,128,1]{0,2,3,1:T(8,128)(2,1)S(1)} %bitcast.197, f32[2,1152,128,8]{2,1,3,0:T(8,128)} %get-tuple-element.535, f32[128,2,8]{0,2,1:T(8,128)S(1)} %select_maximum_fusion.2, pred[128,1152]{0,1:T(8,128)(4,1)S(1)} %compare_select_fusion.7, f32[128,2,8,128]{0,3,2,1:T(8,128)S(1)} %copy-done.3, ...), kind=kOutput, calls=%fused_computation.17.clone.1 | convolution fusion | flops 614203392 | bytes 12288001 | tf_op jit(solution)/shard_map/while/body/eval_jaxpr/rgqk,kgd->rgqd/dot_general | solution.py:131
  205.2 0.9 copy-done.4
  208.7 1.1 compare_select_fusion.7
  209.8 1.3 constant_dynamic-slice_fusion.10
  211.5 5.3 %fusion.92 = (f32[128,2,8]{0,2,1:T(8,128)S(1)}, f32[2,1152,128,8]{2,1,3,0:T(8,128)}) fusion(pred[128,1152]{0,1:T(8,128)(4,1)S(1)} %compare_select_fusion.7, bf16[1152,2,128,1]{0,2,3,1:T(8,128)(2,1)S(1)} %bitcast.196, bf16[128,2,8,128]{3,2,1,0:T(8,128)(2,1)S(1)} %bitcast.194), kind=kOutput, calls=%fused_computation.9.clone.1 | convolution fusion | flops 611055616 | bytes 10706944 | tf_op jit(solution)/shard_map/while/body/eval_jaxpr/rgqd,kgd->rgqk/dot_general | solution.py:123
  216.8 5.6 %fusion.93 = f32[128,2,8]{0,2,1:T(8,128)S(1)} fusion(f32[2,1152,128,8]{2,1,3,0:T(8,128)} %get-tuple-element.535, f32[128,2,8]{0,2,1:T(8,128)S(1)} %select_maximum_fusion.2, pred[128,1152]{0,1:T(8,128)(4,1)S(1)} %compare_select_fusion.7), kind=kLoop, calls=%fused_computation.13.clone.1 | loop fusion | flops 9435136 | bytes 9601024 | tf_op jit(solution)/shard_map/while/body/eval_jaxpr/reduce_sum | solution.py:130
  222.8 5.9 %fusion.95 = f32[128,2,8,128]{0,3,2,1:T(8,128)S(1)} fusion(bf16[1152,2,128,1]{0,2,3,1:T(8,128)(2,1)S(1)} %bitcast.197, f32[2,1152,128,8]{2,1,3,0:T(8,128)} %get-tuple-element.535, f32[128,2,8]{0,2,1:T(8,128)S(1)} %select_maximum_fusion.2, pred[128,1152]{0,1:T(8,128)(4,1)S(1)} %compare_select_fusion.7, f32[128,2,8,128]{0,3,2,1:T(8,128)S(1)} %copy-done.3, ...), kind=kOutput, calls=%fused_computation.17.clone.1 | convolution fusion | flops 614203392 | bytes 12288001 | tf_op jit(solution)/shard_map/while/body/eval_jaxpr/rgqk,kgd->rgqd/dot_general | solution.py:131
  228.7 0.9 copy-done.4
  231.5 0.7 iota_compare_fusion.8
  232.2 1.1 compare_select_fusion.7
  233.3 1.3 constant_dynamic-slice_fusion.10
  235.0 5.3 %fusion.92 = (f32[128,2,8]{0,2,1:T(8,128)S(1)}, f32[2,1152,128,8]{2,1,3,0:T(8,128)}) fusion(pred[128,1152]{0,1:T(8,128)(4,1)S(1)} %compare_select_fusion.7, bf16[1152,2,128,1]{0,2,3,1:T(8,128)(2,1)S(1)} %bitcast.196, bf16[128,2,8,128]{3,2,1,0:T(8,128)(2,1)S(1)} %bitcast.194), kind=kOutput, calls=%fused_computation.9.clone.1 | convolution fusion | flops 611055616 | bytes 10706944 | tf_op jit(solution)/shard_map/while/body/eval_jaxpr/rgqd,kgd->rgqk/dot_general | solution.py:123
  240.3 5.6 %fusion.93 = f32[128,2,8]{0,2,1:T(8,128)S(1)} fusion(f32[2,1152,128,8]{2,1,3,0:T(8,128)} %get-tuple-element.535, f32[128,2,8]{0,2,1:T(8,128)S(1)} %select_maximum_fusion.2, pred[128,1152]{0,1:T(8,128)(4,1)S(1)} %compare_select_fusion.7), kind=kLoop, calls=%fused_computation.13.clone.1 | loop fusion | flops 9435136 | bytes 9601024 | tf_op jit(solution)/shard_map/while/body/eval_jaxpr/reduce_sum | solution.py:130
  246.3 5.9 %fusion.95 = f32[128,2,8,128]{0,3,2,1:T(8,128)S(1)} fusion(bf16[1152,2,128,1]{0,2,3,1:T(8,128)(2,1)S(1)} %bitcast.197, f32[2,1152,128,8]{2,1,3,0:T(8,128)} %get-tuple-element.535, f32[128,2,8]{0,2,1:T(8,128)S(1)} %select_maximum_fusion.2, pred[128,1152]{0,1:T(8,128)(4,1)S(1)} %compare_select_fusion.7, f32[128,2,8,128]{0,3,2,1:T(8,128)S(1)} %copy-done.3, ...), kind=kOutput, calls=%fused_computation.17.clone.1 | convolution fusion | flops 614203392 | bytes 12288001 | tf_op jit(solution)/shard_map/while/body/eval_jaxpr/rgqk,kgd->rgqd/dot_general | solution.py:131
  252.2 0.9 copy-done.4
  255.1 0.7 iota_compare_fusion.8
  255.8 1.1 compare_select_fusion.7
  256.8 1.3 constant_dynamic-slice_fusion.10
  258.6 5.3 %fusion.92 = (f32[128,2,8]{0,2,1:T(8,128)S(1)}, f32[2,1152,128,8]{2,1,3,0:T(8,128)}) fusion(pred[128,1152]{0,1:T(8,128)(4,1)S(1)} %compare_select_fusion.7, bf16[1152,2,128,1]{0,2,3,1:T(8,128)(2,1)S(1)} %bitcast.196, bf16[128,2,8,128]{3,2,1,0:T(8,128)(2,1)S(1)} %bitcast.194), kind=kOutput, calls=%fused_computation.9.clone.1 | convolution fusion | flops 611055616 | bytes 10706944 | tf_op jit(solution)/shard_map/while/body/eval_jaxpr/rgqd,kgd->rgqk/dot_general | solution.py:123
  263.9 5.6 %fusion.93 = f32[128,2,8]{0,2,1:T(8,128)S(1)} fusion(f32[2,1152,128,8]{2,1,3,0:T(8,128)} %get-tuple-element.535, f32[128,2,8]{0,2,1:T(8,128)S(1)} %select_maximum_fusion.2, pred[128,1152]{0,1:T(8,128)(4,1)S(1)} %compare_select_fusion.7), kind=kLoop, calls=%fused_computation.13.clone.1 | loop fusion | flops 9435136 | bytes 9601024 | tf_op jit(solution)/shard_map/while/body/eval_jaxpr/reduce_sum | solution.py:130
  269.8 5.9 %fusion.95 = f32[128,2,8,128]{0,3,2,1:T(8,128)S(1)} fusion(bf16[1152,2,128,1]{0,2,3,1:T(8,128)(2,1)S(1)} %bitcast.197, f32[2,1152,128,8]{2,1,3,0:T(8,128)} %get-tuple-element.535, f32[128,2,8]{0,2,1:T(8,128)S(1)} %select_maximum_fusion.2, pred[128,1152]{0,1:T(8,128)(4,1)S(1)} %compare_select_fusion.7, f32[128,2,8,128]{0,3,2,1:T(8,128)S(1)} %copy-done.3, ...), kind=kOutput, calls=%fused_computation.17.clone.1 | convolution fusion | flops 614203392 | bytes 12288001 | tf_op jit(solution)/shard_map/while/body/eval_jaxpr/rgqk,kgd->rgqd/dot_general | solution.py:131
  275.8 0.9 copy-done.4
  276.7 1.3 broadcast_divide_fusion
  278.3 1.0 select_convert_fusion
  (214 shorter events, 24.7 us)
Async XLA Ops:
  7.2 26.5 %copy-start.2 = (bf16[1,32,2,32,256]{4,3,2,1,0:T(8,128)(2,1)S(1)}, bf16[1,32,2,32,256]{4,3,2,1,0:T(8,128)(2,1)}, u32[]{:S(2)}) copy-start(bf16[1,32,2,32,256]{4,3,2,1,0:T(8,128)(2,1)} %param.18) | copy-start | bytes 3145732
  15.6 32.8 %all-to-all-start = ((bf16[32,2,16,256]{3,2,1,0:T(8,128)(2,1)}), bf16[32,2,16,256]{3,2,1,0:T(8,128)(2,1)S(1)}, u32[]{:S(2)}, u32[]{:S(2)}) async-start(bf16[32,2,16,256]{3,2,1,0:T(8,128)(2,1)} %scatter_fusion), calls=%async_computation | async-start | bytes 1048576 | tf_op jit(solution)/shard_map/all_to_all | solution.py:90
  33.7 23.7 %copy-start.11 = (f32[1,32,512]{2,1,0:T(8,128)S(1)}, f32[1,32,512]{2,1,0:T(8,128)}, u32[]{:S(2)}) copy-start(f32[1,32,512]{2,1,0:T(8,128)} %param.27) | copy-start | bytes 196612
  33.7 23.7 %copy-start.5 = (bf16[1,32,16,512]{3,2,1,0:T(8,128)(2,1)S(1)}, bf16[1,32,16,512]{3,2,1,0:T(8,128)(2,1)}, u32[]{:S(2)}) copy-start(bf16[1,32,16,512]{3,2,1,0:T(8,128)(2,1)} %param.24) | copy-start | bytes 1572868
  33.7 24.0 %copy-start.6 = (bf16[1,2,256,512]{3,2,1,0:T(8,128)(2,1)S(1)}, bf16[1,2,256,512]{3,2,1,0:T(8,128)(2,1)}, u32[]{:S(2)}) copy-start(bf16[1,2,256,512]{3,2,1,0:T(8,128)(2,1)} %param.25) | copy-start | bytes 1572868
  38.8 19.1 %copy-start.7 = (bf16[1,2,256,512]{3,2,1,0:T(8,128)(2,1)S(1)}, bf16[1,2,256,512]{3,2,1,0:T(8,128)(2,1)}, u32[]{:S(2)}) copy-start(bf16[1,2,256,512]{3,2,1,0:T(8,128)(2,1)} %param.26) | copy-start | bytes 1572868
  38.8 19.3 %copy-start.14 = (s32[1,1024]{1,0:T(1,128)S(1)}, s32[1,1024]{1,0:T(1,128)}, u32[]{:S(2)}) copy-start(s32[1,1024]{1,0:T(1,128)} %param.20) | copy-start | bytes 12292
  38.8 19.4 %copy-start.17 = (s32[1,1024]{1,0:T(1,128)S(1)}, s32[1,1024]{1,0:T(1,128)}, u32[]{:S(2)}) copy-start(s32[1,1024]{1,0:T(1,128)} %param.21) | copy-start | bytes 12292
  38.8 25.1 %copy-start.19 = (f32[32]{0:T(128)S(1)}, f32[32]{0:T(128)}, u32[]{:S(2)}) copy-start(f32[32]{0:T(128)} %param.28) | copy-start | bytes 388
  48.4 65.7 %all-to-all-start.1 = ((bf16[32,2,2,32,256]{4,3,2,1,0:T(8,128)(2,1)}), bf16[32,2,2,32,256]{4,3,2,1,0:T(8,128)(2,1)}, u32[]{:S(2)}, u32[]{:S(2)}) async-start(bf16[32,2,2,32,256]{4,3,2,1,0:T(8,128)(2,1)} %scatter_fusion.1), calls=%async_computation.1 | async-start | bytes 4194304 | tf_op jit(solution)/shard_map/all_to_all | solution.py:89
  56.5 125.9 %all-gather.2.cloned.1.call-start = ((), (), s32[]{:S(2)}) async-start(), calls=%async_computation.2 | async-start | bytes 5898240 | tf_op jit(solution)/shard_map/all_gather | solution.py:156
  57.6 61.0 %copy-start.10 = (bf16[1,2,128,256]{3,2,1,0:T(8,128)(2,1)S(1)}, bf16[1,2,128,256]{3,2,1,0:T(8,128)(2,1)}, u32[]{:S(2)}) copy-start(bf16[1,2,128,256]{3,2,1,0:T(8,128)(2,1)} %param.31) | copy-start | bytes 393220
  119.7 62.6 %copy-start.1 = (bf16[1,128,2048]{2,1,0:T(8,128)(2,1)S(1)}, bf16[1,128,2048]{2,1,0:T(8,128)(2,1)}, u32[]{:S(2)}) copy-start(bf16[1,128,2048]{2,1,0:T(8,128)(2,1)} %param.30) | copy-start | bytes 1572868
  119.8 3.3 %copy-start.15 = (f32[32,1]{0,1:T(1,128)}, f32[32,1]{0,1:T(1,128)S(1)}, u32[]{:S(2)}) copy-start(f32[32,1]{0,1:T(1,128)S(1)} %get-tuple-element.564) | copy-start | bytes 388 | tf_op jit(solution)/shard_map/while
  122.9 0.5 copy-start.12
  123.6 1.0 copy-start.8
  123.6 4.1 %copy-start.13 = (f32[32]{0:T(128)S(1)}, f32[32]{0:T(128)}, u32[]{:S(2)}) copy-start(f32[32]{0:T(128)} %copy-done.12) | copy-start | bytes 388 | tf_op jit(solution)/shard_map/while
  127.7 0.8 copy-start.9
  128.7 4.1 %copy-start.16 = (f32[32,1]{0,1:T(1,128)S(1)}, f32[32,1]{0,1:T(1,128)}, u32[]{:S(2)}) copy-start(f32[32,1]{0,1:T(1,128)} %copy-done.15) | copy-start | bytes 388 | tf_op jit(solution)/shard_map/while
  132.8 3.2 %copy-start.15 = (f32[32,1]{0,1:T(1,128)}, f32[32,1]{0,1:T(1,128)S(1)}, u32[]{:S(2)}) copy-start(f32[32,1]{0,1:T(1,128)S(1)} %get-tuple-element.564) | copy-start | bytes 388 | tf_op jit(solution)/shard_map/while
  136.0 0.5 copy-start.12
  136.6 1.0 copy-start.8
  136.6 4.1 %copy-start.13 = (f32[32]{0:T(128)S(1)}, f32[32]{0:T(128)}, u32[]{:S(2)}) copy-start(f32[32]{0:T(128)} %copy-done.12) | copy-start | bytes 388 | tf_op jit(solution)/shard_map/while
  140.8 0.8 copy-start.9
  141.7 4.1 %copy-start.16 = (f32[32,1]{0,1:T(1,128)S(1)}, f32[32,1]{0,1:T(1,128)}, u32[]{:S(2)}) copy-start(f32[32,1]{0,1:T(1,128)} %copy-done.15) | copy-start | bytes 388 | tf_op jit(solution)/shard_map/while
  145.8 3.3 %copy-start.15 = (f32[32,1]{0,1:T(1,128)}, f32[32,1]{0,1:T(1,128)S(1)}, u32[]{:S(2)}) copy-start(f32[32,1]{0,1:T(1,128)S(1)} %get-tuple-element.564) | copy-start | bytes 388 | tf_op jit(solution)/shard_map/while
  149.0 0.5 copy-start.12
  149.7 1.0 copy-start.8
  149.7 4.1 %copy-start.13 = (f32[32]{0:T(128)S(1)}, f32[32]{0:T(128)}, u32[]{:S(2)}) copy-start(f32[32]{0:T(128)} %copy-done.12) | copy-start | bytes 388 | tf_op jit(solution)/shard_map/while
  153.8 0.8 copy-start.9
  154.8 4.1 %copy-start.16 = (f32[32,1]{0,1:T(1,128)S(1)}, f32[32,1]{0,1:T(1,128)}, u32[]{:S(2)}) copy-start(f32[32,1]{0,1:T(1,128)} %copy-done.15) | copy-start | bytes 388 | tf_op jit(solution)/shard_map/while
  158.9 3.3 %copy-start.15 = (f32[32,1]{0,1:T(1,128)}, f32[32,1]{0,1:T(1,128)S(1)}, u32[]{:S(2)}) copy-start(f32[32,1]{0,1:T(1,128)S(1)} %get-tuple-element.564) | copy-start | bytes 388 | tf_op jit(solution)/shard_map/while
  162.0 0.5 copy-start.12
  162.7 1.0 copy-start.8
  162.7 4.1 %copy-start.13 = (f32[32]{0:T(128)S(1)}, f32[32]{0:T(128)}, u32[]{:S(2)}) copy-start(f32[32]{0:T(128)} %copy-done.12) | copy-start | bytes 388 | tf_op jit(solution)/shard_map/while
  166.8 0.8 copy-start.9
  167.8 4.1 %copy-start.16 = (f32[32,1]{0,1:T(1,128)S(1)}, f32[32,1]{0,1:T(1,128)}, u32[]{:S(2)}) copy-start(f32[32,1]{0,1:T(1,128)} %copy-done.15) | copy-start | bytes 388 | tf_op jit(solution)/shard_map/while
  171.9 10.5 %copy-start = (f32[32,16,256]{2,1,0:T(8,128)}, f32[32,16,256]{2,1,0:T(8,128)S(1)}, u32[]{:S(2)}) copy-start(f32[32,16,256]{2,1,0:T(8,128)S(1)} %get-tuple-element.235) | copy-start | bytes 1572868
  182.4 95.9 %copy-start.18 = (pred[128]{0:T(512)(128)(4,1)S(1)}, pred[128]{0:T(512)(128)(4,1)}, u32[]{:S(2)}) copy-start(pred[128]{0:T(512)(128)(4,1)} %add_compare_fusion.1) | copy-start | bytes 388
  193.3 6.0 %copy-start.3 = (f32[128,2,8,128]{0,3,2,1:T(8,128)S(1)}, f32[128,2,8,128]{0,3,2,1:T(8,128)}, u32[]{:S(2)}) copy-start(f32[128,2,8,128]{0,3,2,1:T(8,128)} %get-tuple-element.589) | copy-start | bytes 3145732 | tf_op jit(solution)/shard_map/while
  205.2 1.0 copy-start.4
  216.8 6.0 %copy-start.3 = (f32[128,2,8,128]{0,3,2,1:T(8,128)S(1)}, f32[128,2,8,128]{0,3,2,1:T(8,128)}, u32[]{:S(2)}) copy-start(f32[128,2,8,128]{0,3,2,1:T(8,128)} %get-tuple-element.589) | copy-start | bytes 3145732 | tf_op jit(solution)/shard_map/while
  228.7 1.0 copy-start.4
  240.3 6.0 %copy-start.3 = (f32[128,2,8,128]{0,3,2,1:T(8,128)S(1)}, f32[128,2,8,128]{0,3,2,1:T(8,128)}, u32[]{:S(2)}) copy-start(f32[128,2,8,128]{0,3,2,1:T(8,128)} %get-tuple-element.589) | copy-start | bytes 3145732 | tf_op jit(solution)/shard_map/while
  252.2 1.0 copy-start.4
  263.8 6.0 %copy-start.3 = (f32[128,2,8,128]{0,3,2,1:T(8,128)S(1)}, f32[128,2,8,128]{0,3,2,1:T(8,128)}, u32[]{:S(2)}) copy-start(f32[128,2,8,128]{0,3,2,1:T(8,128)} %get-tuple-element.589) | copy-start | bytes 3145732 | tf_op jit(solution)/shard_map/while
  275.7 1.0 copy-start.4
Sparse Core Ops, SparseCore 0:
  119.8 62.4 all-gather.1
where the time goes:
time: 287 us; the launch traced here: 286 us
  matrix products  79.2 us (28%)
  waiting for transfers between devices  66.2 us (23%)
  local copies, waits for them, and re-layouts  52 us (18%)
  other arithmetic  42.7 us (15%)
  starting transfers between devices  24.6 us (9%)
  between operations  15 us (5%)
  loops' own time  6.46 us (2%)
    all_to_all x1, waiting for transfers between devices, route_blocks(): lax.all_to_all(send_kv, 'pool', split_axis=0, concat_axis=0, tiled=True)  49.6 us
    dot_general x4, matrix products, attend_block(): jnp.einsum('rgqk,kgd->rgqd', weights.astype(jnp.bfloat16), value_heads, p...  23.6 us
    reduce_sum x4, other arithmetic, attend_block(): totals = fade * totals + jnp.sum(weights, axis=-1)  22.6 us
    dot_general x4, matrix products, attend_block(): jnp.einsum('rgqd,kgd->rgqk', query_heads, key_heads, preferred_element_ty...  21.1 us
    all_to_all x1, starting transfers between devices, route_blocks(): lax.all_to_all(send_state, 'pool', split_axis=0, concat_axis=0, tiled=True)  16.5 us
    dot_general x4, matrix products, advance(): jnp.einsum('hps,hns->hpn', value_blk * weights[:, None, :], write_in, pre...  14.5 us
    while x80, local copies, waits for them, and re-layouts  13.7 us
    dot_general x4, matrix products, advance(): jnp.einsum('hpn,hnt->hpt', carried, read_out, precision=exact)  12.3 us
  transfers between devices with their start and end apart: 3, of which 3 were waited for; matrix products, arithmetic and copies ran while one was open for 22% of the time, Pallas kernels for 0%

commit v1 on v0

v1 whole, which is shorter than its diff:
```python
import functools

import jax
import jax.numpy as jnp
from jax import lax
from jax.experimental import pallas as pl
from jax.experimental.pallas import tpu as pltpu
from jax.sharding import PartitionSpec as P

BF = jnp.bfloat16
F32 = jnp.float32
I32 = jnp.int32
MESH = pl.DeviceIdType.MESH

POOL = 32
CTX = 4
PAGES = 32
PAGE = 32
HD = 128
QH = 8
KVH = 2
TOK = 128
TURN = 512
HEADS = 32
CH = 16
STATE = 256
GRP = 2
PER = 16
BLK = 128
HROWS = PAGES * PAGE
ROWS = HROWS + TOK
NEG = -1e30
SCALE = 1.4426950408889634 / (HD**0.5)


def nt(a, b):
    return lax.dot_general(a, b, (((1,), (1,)), ((), ())), preferred_element_type=F32)


def tn(a, b):
    return lax.dot_general(a, b, (((0,), (0,)), ((), ())), preferred_element_type=F32)


def build_tables(own, idx, me, tab_v):
    row = lax.broadcasted_iota(I32, (8, 128), 0)
    lane = lax.broadcasted_iota(I32, (8, 128), 1)
    quarter = lane // 32
    slot = lane % 32
    mine = own == me
    first = jnp.full((8, 128), 99, I32)
    for q in range(4):
        here = quarter == q
        low = jnp.min(jnp.where(here & mine, slot, 99), axis=1, keepdims=True)
        first = jnp.where(here, low, first)
    place = (row * 4 + quarter) * 2 + jnp.where(slot > first, 1, 0)
    place = jnp.where(mine, place, 0)
    block = lax.broadcasted_iota(I32, (PAGES, 128), 0)
    sums = jnp.zeros((PAGES, 128), I32)
    for j in range(PAGES):
        got = jnp.max(jnp.where(idx == j, place, 0), axis=0, keepdims=True)
        sums = jnp.where(block == j, got, sums)
    source = jnp.max(sums, axis=1, keepdims=True)
    local = (row == me // 4) & (quarter == me % 4)
    owners = jnp.sum(jnp.where(local, own + 1, 0), axis=0, keepdims=True) - 1
    wide = lax.broadcasted_iota(I32, (PAGES, 128), 1)
    match = owners == block
    low = jnp.min(jnp.where(match, wide % 32, 31), axis=1, keepdims=True)
    high = jnp.max(jnp.where(match, wide % 32, 0), axis=1, keepdims=True)
    tab_v[...] = jnp.where(wide == 0, low, jnp.where(wide == 1, high, source))


def mixer_local(tlen, rate_s, gain_s, x_v, b_v, c_v, step_v, cum_v, full_v, colw_v, y_v, s_v):
    head = lax.broadcasted_iota(I32, (HEADS, BLK), 0)
    rates = jnp.zeros((HEADS, BLK), F32)
    for h in range(HEADS):
        rates = jnp.where(head == h, rate_s[h], rates)
    up = (
        lax.broadcasted_iota(I32, (BLK, BLK), 0) <= lax.broadcasted_iota(I32, (BLK, BLK), 1)
    )
    ones = jnp.where(up, 1.0, 0.0).astype(F32)
    base = jnp.zeros((HEADS, 1), F32)
    when = lax.broadcasted_iota(I32, (HEADS, BLK), 1)
    for b in range(TURN // BLK):
        cols = slice(b * BLK, (b + 1) * BLK)
        step = jnp.where(when + b * BLK < tlen, step_v[:, cols], 0.0)
        step_v[:, cols] = step
        cum = lax.dot_general(
            -rates * step, ones, (((1,), (0,)), ((), ())),
            preferred_element_type=F32, precision=lax.Precision.HIGHEST,
        )
        cum_v[:, cols] = cum
        full_v[:, cols] = cum + base
        base = base + cum[:, BLK - 1 :]
        padded = jnp.concatenate([cum, jnp.zeros((BLK - HEADS, BLK), F32)], axis=0)
        colw_v[cols, :] = padded.T
    s_v[...] = jnp.zeros_like(s_v)

    def block(b, carry):
        at = pl.ds(pl.multiple_of(b * BLK, BLK), BLK)
        for g in range(GRP):
            bb = b_v[g, :, at]
            cb = c_v[g, :, at]
            pairs = jnp.where(up, tn(bb, cb), 0.0)
            state = s_v[g * PER : (g + 1) * PER].reshape(PER * CH, STATE)
            read = jnp.dot(state.astype(BF), cb, preferred_element_type=F32)
            cums = cum_v[g * PER : (g + 1) * PER, at]
            steps = step_v[g * PER : (g + 1) * PER, at]
            cols = colw_v[at, :]
            late = jnp.exp(cums[:, BLK - 1 :] - cums) * steps
            grow = jnp.exp(cums)
            written = []
            for i in range(PER):
                h = g * PER + i
                xh = x_v[h, :, at].astype(F32)
                gaps = jnp.minimum(cums[i : i + 1] - cols[:, h : h + 1], 0.0)
                mix = (pairs * jnp.exp(gaps)).astype(BF)
                xs = (xh * steps[i : i + 1]).astype(BF)
                y = jnp.dot(xs, mix, preferred_element_type=F32)
                y = y + grow[i : i + 1] * read[i * CH : (i + 1) * CH] + gain_s[h] * xh
                y_v[h, :, at] = y
                written.append((xh * late[i : i + 1]).astype(BF))
            added = nt(jnp.concatenate(written, axis=0), bb)
            for i in range(PER):
                h = g * PER + i
                s_v[h] = grow[i : i + 1, BLK - 1 :] * s_v[h] + added[i * CH : (i + 1) * CH]
        return carry

    lax.fori_loop(0, TURN // BLK, block, 0)


def mixer_saved(tlen, tab_s, saved_v, c_v, full_v, y_v, s_v, mix_o, next_o, s0_v):
    def pick(j, carry):
        s0_v[j] = saved_v[tab_s[j, 2]]
        return carry

    lax.fori_loop(0, HEADS, pick, 0)
    when = lax.broadcasted_iota(I32, (CH, TURN), 1)
    for g in range(GRP):
        start = s0_v[g * PER : (g + 1) * PER].reshape(PER * CH, STATE)
        read = jnp.dot(start, c_v[g], preferred_element_type=F32)
        for i in range(PER):
            h = g * PER + i
            grow = jnp.exp(full_v[h : h + 1, :])
            y = y_v[h] + grow * read[i * CH : (i + 1) * CH]
            mix_o[h] = jnp.where(when < tlen, y, 0.0).astype(BF)
            last = grow[:, TURN - 1 :]
            next_o[h] = last * s0_v[h].astype(F32) + s_v[h]


def attend(g, hlen, seg, q_all, k_v, v_v, o_send, l_send, send_part):
    key = lax.broadcasted_iota(I32, (1, HROWS), 1) + seg * HROWS
    seen = jnp.where(key < hlen, 0.0, NEG)
    half = QH // 2
    lane = lax.broadcasted_iota(I32, (TOK, 128), 1)

    def dest(k, carry):
        off = lax.rem(k + 1, CTX)
        c = lax.rem(seg + off, CTX)
        token = lax.broadcasted_iota(I32, (TOK, TOK), 0) + c * TOK
        fresh = lax.broadcasted_iota(I32, (TOK, TOK), 1) + seg * TOK
        turn = jnp.where(fresh <= token, 0.0, NEG)
        turn = jnp.concatenate([turn] * half, axis=0)
        keep = jnp.zeros((TOK, 128), F32)
        for part in range(2):
            first = g * QH + part * half
            q = jnp.concatenate(
                [q_all[c, :, (first + j) * HD : (first + j + 1) * HD] for j in range(half)], axis=0
            )
            s = nt(q, k_v[...]) * SCALE
            sh = s[:, :HROWS] + seen
            st = s[:, HROWS:] + turn
            top = jnp.maximum(
                jnp.max(sh, axis=1, keepdims=True), jnp.max(st, axis=1, keepdims=True)
            )
            ph = jnp.exp2(sh - top).astype(BF)
            pt = jnp.exp2(st - top).astype(BF)
            o = jnp.dot(ph, v_v[:HROWS], preferred_element_type=F32) + jnp.dot(
                pt, v_v[HROWS:], preferred_element_type=F32
            )
            total = o[:, HD:]
            out = (o[:, :HD] / total).astype(BF)
            logs = top + jnp.log2(total)
            for j in range(half):
                at = slice(j * TOK, (j + 1) * TOK)
                n = part * half + j
                o_send[g, k, :, n * HD : (n + 1) * HD] = out[at]
                keep = jnp.where(lane == n, logs[at], keep)
        l_send[g, k] = keep.T[:QH]

        @pl.when(k < CTX - 1)
        def _():
            send_part(g, k, off, c)

        return carry

    lax.fori_loop(0, CTX, dest, 0)


def merge(g, tlen, seg, o_send, l_send, o_recv, l_recv, att_o):
    logs = [l_recv[g, 0], l_recv[g, 1], l_recv[g, 2], l_send[g, CTX - 1]]
    top = functools.reduce(jnp.maximum, logs)
    parts = [jnp.exp2(l - top) for l in logs]
    whole = parts[0] + parts[1] + parts[2] + parts[3]
    shares = jnp.concatenate(
        [p / whole for p in parts] + [jnp.zeros((TOK - CTX * QH, 128), F32)], axis=0
    ).T
    live = lax.broadcasted_iota(I32, (TOK, HD), 0) + seg * TOK < tlen
    for j in range(QH):
        cols = slice(j * HD, (j + 1) * HD)
        out = jnp.zeros((TOK, HD), F32)
        for i in range(CTX):
            part = o_recv[g, i, :, cols] if i < CTX - 1 else o_send[g, CTX - 1, :, cols]
            n = i * QH + j
            out = out + shares[:, n : n + 1] * part.astype(F32)
        base = g * QH * HD
        att_o[:, base + j * HD : base + (j + 1) * HD] = jnp.where(live, out, 0.0).astype(BF)


def kernel(
    hlen_s, tlen_s, rate_s, gain_s, own_r, idx_r,
    kv_h, st_h, x_h, b_h, c_h, step_h, q_h, turn_h,
    mix_o, next_o, att_o,
    kv_v, st_v, x_v, b_v, c_v, step_v, turn_v, tab_v, tab_s,
    kv_send, kv_recv0, kv_recv1, st_send, st_recv, q_all,
    cum_v, full_v, colw_v, y_v, s_v, s0_v, k_v, v_v,
    o_send, l_send, o_recv, l_recv,
    in_sem, tab_sem, kv_ss, kv_rs, st_ss, st_rs, q_ss, q_rs, o_ss, o_rs, l_ss, l_rs,
):
    me = lax.axis_index("pool")
    seg = lax.axis_index("ctx")
    side = lax.axis_index("head")
    row, col = me // 8, me % 8
    hlen, tlen = hlen_s[0], tlen_s[0]
    kv_recv = (kv_recv0, kv_recv1)

    def peer(i):
        k = lax.rem(i * 11, POOL)
        return lax.rem(row + k // 8, 4) * 8 + lax.rem(col + lax.rem(k, 8), 8)

    loads = [
        pltpu.make_async_copy(src, dst, in_sem.at[i])
        for i, (src, dst) in enumerate(
            [
                (kv_h, kv_v), (st_h, st_v), (q_h, q_all.at[seg]), (x_h, x_v), (b_h, b_v),
                (c_h, c_v), (step_h, step_v), (turn_h, turn_v),
            ]
        )
    ]
    for load in loads:
        load.start()

    barrier = pltpu.get_barrier_semaphore()

    def greet(i, carry):
        pl.semaphore_signal(
            barrier, inc=1, device_id=(peer(i), seg, side), device_id_type=MESH
        )
        return carry

    lax.fori_loop(1, POOL, greet, 0)
    for off in range(1, CTX):
        pl.semaphore_signal(
            barrier, inc=1, device_id=(me, lax.rem(seg + off, CTX), side), device_id_type=MESH
        )
    build_tables(own_r[...], idx_r[...], me, tab_v)
    table = pltpu.make_async_copy(tab_v, tab_s, tab_sem)
    table.start()
    table.wait()
    loads[0].wait()
    pl.semaphore_wait(barrier, POOL - 1 + CTX - 1)

    def kv_copy(g, i):
        return pltpu.make_async_remote_copy(
            src_ref=kv_send.at[g, pl.ds(2 * i, 2)], dst_ref=kv_recv[g].at[pl.ds(2 * me, 2)],
            send_sem=kv_ss.at[g, i], recv_sem=kv_rs.at[g, i],
            device_id=(peer(i), seg, side), device_id_type=MESH,
        )

    def st_copy(i):
        return pltpu.make_async_remote_copy(
            src_ref=st_send.at[pl.ds(2 * i, 2)], dst_ref=st_recv.at[pl.ds(2 * me, 2)],
            send_sem=st_ss.at[i], recv_sem=st_rs.at[i],
            device_id=(peer(i), seg, side), device_id_type=MESH,
        )

    def q_copy(g, off):
        cols = pl.ds(g * QH * HD, QH * HD)
        return pltpu.make_async_remote_copy(
            src_ref=q_h.at[:, cols], dst_ref=q_all.at[seg, :, cols],
            send_sem=q_ss.at[g, off - 1], recv_sem=q_rs.at[g, off - 1],
            device_id=(me, lax.rem(seg + off, CTX), side), device_id_type=MESH,
        )

    for g in range(KVH):
        lanes = slice(g * HD, (g + 1) * HD)
        for r in range(2):
            kv_recv[g][2 * me + r] = kv_v[tab_s[me, r], :, :, lanes]

        def pack(i, carry):
            to = peer(i)
            for r in range(2):
                kv_send[g, 2 * i + r] = kv_v[tab_s[to, r], :, :, lanes]
            kv_copy(g, i).start()
            return carry

        lax.fori_loop(1, POOL, pack, 0)
        for off in range(1, CTX):
            q_copy(g, off).start()
    loads[1].wait()
    for r in range(2):
        st_recv[2 * me + r] = st_v[tab_s[me, r]]

    def pack_state(i, carry):
        to = peer(i)
        for r in range(2):
            st_send[2 * i + r] = st_v[tab_s[to, r]]
        st_copy(i).start()
        return carry

    lax.fori_loop(1, POOL, pack_state, 0)

    for load in loads[2:]:
        load.wait()
    mixer_local(tlen, rate_s, gain_s, x_v, b_v, c_v, step_v, cum_v, full_v, colw_v, y_v, s_v)

    v_v[:, HD:] = jnp.ones((ROWS, HD), BF)

    def o_copy(g, k, off, c):
        return pltpu.make_async_remote_copy(
            src_ref=o_send.at[g, k], dst_ref=o_recv.at[g, k],
            send_sem=o_ss.at[g, k], recv_sem=o_rs.at[g, k],
            device_id=(me, c, side), device_id_type=MESH,
        )

    def l_copy(g, k, off, c):
        return pltpu.make_async_remote_copy(
            src_ref=l_send.at[g, k], dst_ref=l_recv.at[g, k],
            send_sem=l_ss.at[g, k], recv_sem=l_rs.at[g, k],
            device_id=(me, c, side), device_id_type=MESH,
        )

    def send_part(g, k, off, c):
        o_copy(g, k, off, c).start()
        l_copy(g, k, off, c).start()

    for g in range(KVH):
        lanes = slice(g * HD, (g + 1) * HD)

        def arrive(i, carry):
            kv_copy(g, i).wait_recv()
            return carry

        lax.fori_loop(1, POOL, arrive, 0)

        def place(j, carry):
            page = kv_recv[g][tab_s[j, 2]]
            at = pl.ds(pl.multiple_of(j * PAGE, PAGE), PAGE)
            k_v[at, :] = page[0]
            v_v[at, :HD] = page[1]
            return carry

        lax.fori_loop(0, PAGES, place, 0)
        k_v[HROWS:, :] = turn_v[0, :, lanes]
        v_v[HROWS:, :HD] = turn_v[1, :, lanes]
        for off in range(1, CTX):
            q_copy(g, off).wait_recv()
        attend(g, hlen, seg, q_all, k_v, v_v, o_send, l_send, send_part)

    def state_arrives(i, carry):
        st_copy(i).wait_recv()
        return carry

    lax.fori_loop(1, POOL, state_arrives, 0)
    mixer_saved(tlen, tab_s, st_recv, c_v, full_v, y_v, s_v, mix_o, next_o, s0_v)

    for g in range(KVH):
        for k in range(CTX - 1):
            off = k + 1
            c = lax.rem(seg + off, CTX)
            o_copy(g, k, off, c).wait_recv()
            l_copy(g, k, off, c).wait_recv()
        merge(g, tlen, seg, o_send, l_send, o_recv, l_recv, att_o)

    def drain(i, carry):
        for g in range(KVH):
            kv_copy(g, i).wait_send()
        st_copy(i).wait_send()
        return carry

    lax.fori_loop(1, POOL, drain, 0)
    for g in range(KVH):
        for k in range(CTX - 1):
            off = k + 1
            c = lax.rem(seg + off, CTX)
            q_copy(g, off).wait_send()
            o_copy(g, k, off, c).wait_send()
            l_copy(g, k, off, c).wait_send()


def local(
    kv_pool, state_pool, block_owner, block_index, history_len, turn_len, mixer_in, input_proj,
    output_proj, step_size, decay_rate, bypass_factor, queries, turn_kv,
):
    hbm = pl.BlockSpec(memory_space=pl.ANY)
    vmem = pl.BlockSpec(memory_space=pltpu.VMEM)
    smem = pl.BlockSpec(memory_space=pltpu.SMEM)
    dma = pltpu.SemaphoreType.DMA
    mixed, final, attended = pl.pallas_call(
        kernel,
        out_shape=(
            jax.ShapeDtypeStruct((HEADS, CH, TURN), BF),
            jax.ShapeDtypeStruct((HEADS, CH, STATE), F32),
            jax.ShapeDtypeStruct((TOK, KVH * QH * HD), BF),
        ),
        in_specs=[smem] * 4 + [vmem] * 2 + [hbm] * 8,
        out_specs=(vmem, vmem, vmem),
        scratch_shapes=[
            pltpu.VMEM((PAGES, 2, PAGE, KVH * HD), BF),
            pltpu.VMEM((PAGES, CH, STATE), BF),
            pltpu.VMEM((HEADS, CH, TURN), BF),
            pltpu.VMEM((GRP, STATE, TURN), BF),
            pltpu.VMEM((GRP, STATE, TURN), BF),
            pltpu.VMEM((HEADS, TURN), F32),
            pltpu.VMEM((2, TOK, KVH * HD), BF),
            pltpu.VMEM((PAGES, 128), I32),
            pltpu.SMEM((PAGES, 128), I32),
            pltpu.VMEM((KVH, 2 * POOL, 2, PAGE, HD), BF),
            pltpu.VMEM((2 * POOL, 2, PAGE, HD), BF),
            pltpu.VMEM((2 * POOL, 2, PAGE, HD), BF),
            pltpu.VMEM((2 * POOL, CH, STATE), BF),
            pltpu.VMEM((2 * POOL, CH, STATE), BF),
            pltpu.VMEM((CTX, TOK, KVH * QH * HD), BF),
            pltpu.VMEM((HEADS, TURN), F32),
            pltpu.VMEM((HEADS, TURN), F32),
            pltpu.VMEM((TURN, 128), F32),
            pltpu.VMEM((HEADS, CH, TURN), F32),
            pltpu.VMEM((HEADS, CH, STATE), F32),
            pltpu.VMEM((HEADS, CH, STATE), BF),
            pltpu.VMEM((ROWS, HD), BF),
            pltpu.VMEM((ROWS, 2 * HD), BF),
            pltpu.VMEM((KVH, CTX, TOK, QH * HD), BF),
            pltpu.VMEM((KVH, CTX, QH, TOK), F32),
            pltpu.VMEM((KVH, CTX - 1, TOK, QH * HD), BF),
            pltpu.VMEM((KVH, CTX - 1, QH, TOK), F32),
            dma((8,)), dma(()),
            dma((KVH, POOL)), dma((KVH, POOL)), dma((POOL,)), dma((POOL,)),
            dma((KVH, CTX - 1)), dma((KVH, CTX - 1)), dma((KVH, CTX - 1)), dma((KVH, CTX - 1)),
            dma((KVH, CTX - 1)), dma((KVH, CTX - 1)),
        ],
        compiler_params=pltpu.CompilerParams(
            collective_id=0, has_side_effects=True, vmem_limit_bytes=56 << 20
        ),
        name="resume",
    )(
        history_len, turn_len, decay_rate, bypass_factor,
        block_owner.reshape(8, 128), block_index.reshape(8, 128),
        kv_pool[0], state_pool, mixer_in[0], input_proj[0], output_proj[0], step_size[0],
        queries[0], turn_kv[0],
    )
    return mixed[None], final[None], attended[None]


def solution(mesh):
    return jax.shard_map(
        local,
        mesh=mesh,
        in_specs=(
            P("ctx", "pool", None, None, "head"),
            P("pool", "ctx", "head"),
            P("ctx", None),
            P("ctx", None),
            P("pool"),
            P("pool"),
            P("pool", "head", "ctx", None),
            P("pool", "head", None, None),
            P("pool", "head", None, None),
            P("pool", "head", None),
            P("head"),
            P("head"),
            P("pool", "ctx", "head"),
            P("pool", None, "ctx", "head"),
        ),
        out_specs=(
            P("pool", "head", "ctx", None),
            P("pool", "head", "ctx", None),
            P("pool", "ctx", "head"),
        ),
        check_vma=False,
    )
```

time: 287 us -> 108 us (0.38)
  the two profiles are of different devices: /device:TPU:1 before, /device:TPU:16 now
where the time goes in v1:
time: 108 us
  Pallas kernels  102 us (94%)
  local copies, waits for them, and re-layouts  3.95 us (4%)
  between operations  1.94 us (2%)
    pallas_call x1, Pallas kernels, local(): pl.pallas_call(kernel, out_shape=(jax.ShapeDtypeStruct((HEADS, CH, TURN),...  102 us
    unnamed x7, local copies, waits for them, and re-layouts  3.95 us

profile of v1, /device:TPU:16, one launch (start us, length us, event | category | flops | bytes accessed | tf_op | source)
XLA Modules:
  0.0 108.2 jit_solution(16674651024420846280)
XLA Ops:
  1.9 102.3 %resume.1 = (bf16[32,16,512]{2,1,0:T(8,128)(2,1)}, f32[32,16,256]{2,1,0:T(8,128)}, bf16[128,2048]{1,0:T(8,128)(2,1)}) custom-call(s32[1]{0:T(128)S(6)} %copy.20.hlen_s, s32[1]{0:T(128)S(6)} %copy.21.tlen_s, f32[32]{0:T(128)} %rate_s.1, f32[32]{0:T(128)} %gain_s.1, s32[8,128]{1,0:T(8,128)} %bitcast.22, s32[8,128]{1,0:T(8,128)} %bitcast.23, ...), custom_call_target="tpu_custom_call" | custom-call | tf_op jit(solution)/shard_map/resume/pallas_call | solution.py:408
  104.2 0.0 copy-start.1
  104.2 1.9 %copy.22 = bf16[1,32,16,512]{3,2,1,0:T(8,128)(2,1)} copy(bf16[1,32,16,512]{3,2,1,0:T(8,128)(2,1)} %bitcast.19) | data formatting | bytes 1048576
  106.2 0.0 copy-done.1
  106.2 0.0 copy-start
  106.2 0.8 copy.23
  107.0 0.4 copy-done
  107.4 0.8 copy.24
Async XLA Ops:
  104.2 1.9 %copy-start.1 = (f32[32,16,256]{2,1,0:T(8,128)S(1)}, f32[32,16,256]{2,1,0:T(8,128)}, u32[]{:S(2)}) copy-start(f32[32,16,256]{2,1,0:T(8,128)} %get-tuple-element.7) | copy-start | bytes 1572868
  106.2 1.2 %copy-start = (bf16[128,2048]{1,0:T(8,128)(2,1)S(1)}, bf16[128,2048]{1,0:T(8,128)(2,1)}, u32[]{:S(2)}) copy-start(bf16[128,2048]{1,0:T(8,128)(2,1)} %get-tuple-element.8) | copy-start | bytes 1572868

commit v2 on v1

--- a/solution.py
+++ b/solution.py
@@ -217,10 +217,10 @@
 
 
 def kernel(
-    hlen_s, tlen_s, rate_s, gain_s, own_r, idx_r,
+    rate_s, gain_s, own_r, idx_r, hlen_h, tlen_h,
     kv_h, st_h, x_h, b_h, c_h, step_h, q_h, turn_h,
     mix_o, next_o, att_o,
-    kv_v, st_v, x_v, b_v, c_v, step_v, turn_v, tab_v, tab_s,
+    hlen_s, tlen_s, kv_v, st_v, x_v, b_v, c_v, step_v, turn_v, tab_v, tab_s,
     kv_send, kv_recv0, kv_recv1, st_send, st_recv, q_all,
     cum_v, full_v, colw_v, y_v, s_v, s0_v, k_v, v_v,
     o_send, l_send, o_recv, l_recv,
@@ -230,44 +230,40 @@
     seg = lax.axis_index("ctx")
     side = lax.axis_index("head")
     row, col = me // 8, me % 8
-    hlen, tlen = hlen_s[0], tlen_s[0]
     kv_recv = (kv_recv0, kv_recv1)
 
     def peer(i):
-        k = lax.rem(i * 11, POOL)
+        k = lax.rem(i * jnp.where(side % 2 == 0, 11, 21), POOL)
         return lax.rem(row + k // 8, 4) * 8 + lax.rem(col + lax.rem(k, 8), 8)
+
+    barrier = pltpu.get_barrier_semaphore()
+
+    def greet(i, carry):
+        pl.semaphore_signal(
+            barrier, inc=1, device_id=(peer(i), seg, side), device_id_type=MESH
+        )
+        return carry
+
+    lax.fori_loop(1, POOL, greet, 0)
+    for off in range(1, CTX):
+        pl.semaphore_signal(
+            barrier, inc=1, device_id=(me, lax.rem(seg + off, CTX), side), device_id_type=MESH
+        )
 
     loads = [
         pltpu.make_async_copy(src, dst, in_sem.at[i])
         for i, (src, dst) in enumerate(
             [
                 (kv_h, kv_v), (st_h, st_v), (q_h, q_all.at[seg]), (x_h, x_v), (b_h, b_v),
-                (c_h, c_v), (step_h, step_v), (turn_h, turn_v),
+                (c_h, c_v), (step_h, step_v), (turn_h, turn_v), (hlen_h, hlen_s), (tlen_h, tlen_s),
             ]
         )
     ]
     for load in loads:
         load.start()
-
-    barrier = pltpu.get_barrier_semaphore()
-
-    def greet(i, carry):
-        pl.semaphore_signal(
-            barrier, inc=1, device_id=(peer(i), seg, side), device_id_type=MESH
-        )
-        return carry
-
-    lax.fori_loop(1, POOL, greet, 0)
-    for off in range(1, CTX):
-        pl.semaphore_signal(
-            barrier, inc=1, device_id=(me, lax.rem(seg + off, CTX), side), device_id_type=MESH
-        )
     build_tables(own_r[...], idx_r[...], me, tab_v)
     table = pltpu.make_async_copy(tab_v, tab_s, tab_sem)
     table.start()
-    table.wait()
-    loads[0].wait()
-    pl.semaphore_wait(barrier, POOL - 1 + CTX - 1)
 
     def kv_copy(g, i):
         return pltpu.make_async_remote_copy(
@@ -291,110 +287,136 @@
             device_id=(me, lax.rem(seg + off, CTX), side), device_id_type=MESH,
         )
 
-    for g in range(KVH):
+    def o_copy(g, k, c):
+        return pltpu.make_async_remote_copy(
+            src_ref=o_send.at[g, k], dst_ref=o_recv.at[g, k],
+            send_sem=o_ss.at[g, k], recv_sem=o_rs.at[g, k],
+            device_id=(me, c, side), device_id_type=MESH,
+        )
+
+    def l_copy(g, k, c):
+        return pltpu.make_async_remote_copy(
+            src_ref=l_send.at[g, k], dst_ref=l_recv.at[g, k],
+            send_sem=l_ss.at[g, k], recv_sem=l_rs.at[g, k],
+            device_id=(me, c, side), device_id_type=MESH,
+        )
+
+    def send_part(g, k, off, c):
+        o_copy(g, k, c).start()
+        l_copy(g, k, c).start()
+
+    def pack_kv(g):
         lanes = slice(g * HD, (g + 1) * HD)
-        for r in range(2):
-            kv_recv[g][2 * me + r] = kv_v[tab_s[me, r], :, :, lanes]
 
         def pack(i, carry):
             to = peer(i)
             for r in range(2):
                 kv_send[g, 2 * i + r] = kv_v[tab_s[to, r], :, :, lanes]
-            kv_copy(g, i).start()
             return carry
 
         lax.fori_loop(1, POOL, pack, 0)
-        for off in range(1, CTX):
-            q_copy(g, off).start()
-    loads[1].wait()
-    for r in range(2):
-        st_recv[2 * me + r] = st_v[tab_s[me, r]]
-
-    def pack_state(i, carry):
-        to = peer(i)
         for r in range(2):
-            st_send[2 * i + r] = st_v[tab_s[to, r]]
-        st_copy(i).start()
-        return carry
-
-    lax.fori_loop(1, POOL, pack_state, 0)
-
-    for load in loads[2:]:
-        load.wait()
-    mixer_local(tlen, rate_s, gain_s, x_v, b_v, c_v, step_v, cum_v, full_v, colw_v, y_v, s_v)
-
-    v_v[:, HD:] = jnp.ones((ROWS, HD), BF)
-
-    def o_copy(g, k, off, c):
-        return pltpu.make_async_remote_copy(
-            src_ref=o_send.at[g, k], dst_ref=o_recv.at[g, k],
-            send_sem=o_ss.at[g, k], recv_sem=o_rs.at[g, k],
-            device_id=(me, c, side), device_id_type=MESH,
-        )
-
-    def l_copy(g, k, off, c):
-        return pltpu.make_async_remote_copy(
-            src_ref=l_send.at[g, k], dst_ref=l_recv.at[g, k],
-            send_sem=l_ss.at[g, k], recv_sem=l_rs.at[g, k],
-            device_id=(me, c, side), device_id_type=MESH,
-        )
-
-    def send_part(g, k, off, c):
-        o_copy(g, k, off, c).start()
-        l_copy(g, k, off, c).start()
-
-    for g in range(KVH):
+            kv_recv[g][2 * me + r] = kv_v[tab_s[me, r], :, :, lanes]
+
+    def each(body, first=1, last=POOL):
+        def step(i, carry):
+            body(i)
+            return carry
+
+        lax.fori_loop(first, last, step, 0)
+
+    def arrive_kv(g):
         lanes = slice(g * HD, (g + 1) * HD)
-
-        def arrive(i, carry):
-            kv_copy(g, i).wait_recv()
-            return carry
-
-        lax.fori_loop(1, POOL, arrive, 0)
-
-        def place(j, carry):
+        if g == 0:
+            each(lambda i: kv_copy(g, i).wait_recv())
+
+        def place(j):
             page = kv_recv[g][tab_s[j, 2]]
             at = pl.ds(pl.multiple_of(j * PAGE, PAGE), PAGE)
             k_v[at, :] = page[0]
             v_v[at, :HD] = page[1]
-            return carry
-
-        lax.fori_loop(0, PAGES, place, 0)
+
+        each(place, 0, PAGES)
         k_v[HROWS:, :] = turn_v[0, :, lanes]
         v_v[HROWS:, :HD] = turn_v[1, :, lanes]
         for off in range(1, CTX):
             q_copy(g, off).wait_recv()
-        attend(g, hlen, seg, q_all, k_v, v_v, o_send, l_send, send_part)
-
-    def state_arrives(i, carry):
-        st_copy(i).wait_recv()
-        return carry
-
-    lax.fori_loop(1, POOL, state_arrives, 0)
+
+    def join(g):
+        for k in range(CTX - 1):
+            c = lax.rem(seg + k + 1, CTX)
+            o_copy(g, k, c).wait_recv()
+            l_copy(g, k, c).wait_recv()
+        merge(g, tlen_s[0], seg, o_send, l_send, o_recv, l_recv, att_o)
+
+    table.wait()
+    loads[0].wait()
+    pack_kv(0)
+    pl.semaphore_wait(barrier, POOL - 1 + CTX - 1)
+    each(lambda i: kv_copy(0, i).start())
+    for off in range(1, CTX):
+        q_copy(0, off).start()
+    for off in range(1, CTX):
+        q_copy(1, off).start()
+    pack_kv(1)
+    loads[1].wait()
+    for r in range(2):
+        st_recv[2 * me + r] = st_v[tab_s[me, r]]
+
+    def pack_state(i):
+        to = peer(i)
+        for r in range(2):
+            st_send[2 * i + r] = st_v[tab_s[to, r]]
+
+    each(lambda i: kv_copy(1, i).start())
+    each(pack_state)
+    for load in loads[2:]:
+        load.wait()
+    hlen, tlen = hlen_s[0], tlen_s[0]
+    mixer_local(tlen, rate_s, gain_s, x_v, b_v, c_v, step_v, cum_v, full_v, colw_v, y_v, s_v)
+    v_v[:, HD:] = jnp.ones((ROWS, HD), BF)
+
+    def second(i):
+        kv_copy(0, i).wait_send()
+        kv_copy(1, i).start()
+
+    arrive_kv(0)
+    attend(0, hlen, seg, q_all, k_v, v_v, o_send, l_send, send_part)
+
+    def third(i):
+        kv_copy(1, i).wait_send()
+        st_copy(i).start()
+
+    each(lambda i: kv_copy(1, i).wait_recv())
+    each(third)
+    arrive_kv(1)
+    attend(1, hlen, seg, q_all, k_v, v_v, o_send, l_send, send_part)
+    join(0)
+    each(lambda i: st_copy(i).wait_recv())
     mixer_saved(tlen, tab_s, st_recv, c_v, full_v, y_v, s_v, mix_o, next_o, s0_v)
-
+    join(1)
+
+    each(lambda i: st_copy(i).wait_send())
+    each(lambda i: kv_copy(0, i).wait_send())
     for g in range(KVH):
         for k in range(CTX - 1):
-            off = k + 1
-            c = lax.rem(seg + off, CTX)
-            o_copy(g, k, off, c).wait_recv()
-            l_copy(g, k, off, c).wait_recv()
-        merge(g, tlen, seg, o_send, l_send, o_recv, l_recv, att_o)
-
-    def drain(i, carry):
-        for g in range(KVH):
-            kv_copy(g, i).wait_send()
-        st_copy(i).wait_send()
-        return carry
-
-    lax.fori_loop(1, POOL, drain, 0)
-    for g in range(KVH):
-        for k in range(CTX - 1):
-            off = k + 1
-            c = lax.rem(seg + off, CTX)
-            q_copy(g, off).wait_send()
-            o_copy(g, k, off, c).wait_send()
-            l_copy(g, k, off, c).wait_send()
+            c = lax.rem(seg + k + 1, CTX)
+            q_copy(g, k + 1).wait_send()
+            o_copy(g, k, c).wait_send()
+            l_copy(g, k, c).wait_send()
+
+
+def hand_over(a, b, c, x, y, z, u, v, w, sem):
+    trips = [(a, u, x), (b, v, y), (c, w, z)]
+    there = [pltpu.make_async_copy(src, mid, sem.at[0, i]) for i, (src, mid, _) in enumerate(trips)]
+    back = [pltpu.make_async_copy(mid, dst, sem.at[1, i]) for i, (_, mid, dst) in enumerate(trips)]
+    for copy in there:
+        copy.start()
+    for first, then in zip(there, back):
+        first.wait()
+        then.start()
+    for copy in back:
+        copy.wait()
 
 
 def local(
@@ -405,16 +427,19 @@
     vmem = pl.BlockSpec(memory_space=pltpu.VMEM)
     smem = pl.BlockSpec(memory_space=pltpu.SMEM)
     dma = pltpu.SemaphoreType.DMA
-    mixed, final, attended = pl.pallas_call(
+    outs = (
+        jax.ShapeDtypeStruct((HEADS, CH, TURN), BF),
+        jax.ShapeDtypeStruct((HEADS, CH, STATE), F32),
+        jax.ShapeDtypeStruct((TOK, KVH * QH * HD), BF),
+    )
+    results = pl.pallas_call(
         kernel,
-        out_shape=(
-            jax.ShapeDtypeStruct((HEADS, CH, TURN), BF),
-            jax.ShapeDtypeStruct((HEADS, CH, STATE), F32),
-            jax.ShapeDtypeStruct((TOK, KVH * QH * HD), BF),
-        ),
-        in_specs=[smem] * 4 + [vmem] * 2 + [hbm] * 8,
+        out_shape=outs,
+        in_specs=[smem] * 2 + [vmem] * 2 + [pl.BlockSpec(memory_space=pltpu.HBM)] * 2 + [hbm] * 8,
         out_specs=(vmem, vmem, vmem),
         scratch_shapes=[
+            pltpu.SMEM((1,), I32),
+            pltpu.SMEM((1,), I32),
             pltpu.VMEM((PAGES, 2, PAGE, KVH * HD), BF),
             pltpu.VMEM((PAGES, CH, STATE), BF),
             pltpu.VMEM((HEADS, CH, TURN), BF),
@@ -442,7 +467,7 @@
             pltpu.VMEM((KVH, CTX, QH, TOK), F32),
             pltpu.VMEM((KVH, CTX - 1, TOK, QH * HD), BF),
             pltpu.VMEM((KVH, CTX - 1, QH, TOK), F32),
-            dma((8,)), dma(()),
+            dma((10,)), dma(()),
             dma((KVH, POOL)), dma((KVH, POOL)), dma((POOL,)), dma((POOL,)),
             dma((KVH, CTX - 1)), dma((KVH, CTX - 1)), dma((KVH, CTX - 1)), dma((KVH, CTX - 1)),
             dma((KVH, CTX - 1)), dma((KVH, CTX - 1)),
@@ -452,11 +477,19 @@
         ),
         name="resume",
     )(
-        history_len, turn_len, decay_rate, bypass_factor,
-        block_owner.reshape(8, 128), block_index.reshape(8, 128),
+        decay_rate, bypass_factor,
+        block_owner.reshape(8, 128), block_index.reshape(8, 128), history_len, turn_len,
         kv_pool[0], state_pool, mixer_in[0], input_proj[0], output_proj[0], step_size[0],
         queries[0], turn_kv[0],
     )
+    mixed, final, attended = pl.pallas_call(
+        hand_over,
+        out_shape=outs,
+        in_specs=[hbm] * 3,
+        out_specs=(hbm,) * 3,
+        scratch_shapes=[pltpu.VMEM(o.shape, o.dtype) for o in outs] + [dma((2, 3))],
+        name="hand_over",
+    )(*results)
     return mixed[None], final[None], attended[None]
 
 

time: 108 us -> 94.8 us (0.88)
  the two profiles are of different devices: /device:TPU:16 before, /device:TPU:1 now
where the time goes in v2:
time: 94.8 us; the launch traced here: 93.2 us
  Pallas kernels  91.3 us (96%)
  between operations  1.93 us (2%)
    pallas_call x1, Pallas kernels, local(): pl.pallas_call(kernel, out_shape=outs, in_specs=[smem] * 2 + [vmem] * 2 +...  89 us
    pallas_call x1, Pallas kernels, local(): pl.pallas_call(hand_over, out_shape=outs, in_specs=[hbm] * 3, out_specs=(...  2.23 us

profile of v2, /device:TPU:1, one launch (start us, length us, event | category | flops | bytes accessed | tf_op | source)
XLA Modules:
  0.0 93.2 jit_solution(12674757607741747715)
XLA Ops:
  1.9 89.0 %resume.1 = (bf16[32,16,512]{2,1,0:T(8,128)(2,1)}, f32[32,16,256]{2,1,0:T(8,128)}, bf16[128,2048]{1,0:T(8,128)(2,1)}) custom-call(f32[32]{0:T(128)} %rate_s.1, f32[32]{0:T(128)} %gain_s.1, s32[8,128]{1,0:T(8,128)} %bitcast.19, s32[8,128]{1,0:T(8,128)} %bitcast.20, s32[1]{0:T(128)S(6)} %copy.17.hlen_h, s32[1]{0:T(128)S(6)} %copy.18.tlen_h, ...), custom_call_target="tpu_custom_call" | custom-call | tf_op jit(solution)/shard_map/resume/pallas_call | solution.py:435
  91.0 2.2 %hand_over.1 = (bf16[32,16,512]{2,1,0:T(8,128)(2,1)}, f32[32,16,256]{2,1,0:T(8,128)}, bf16[128,2048]{1,0:T(8,128)(2,1)}) custom-call(bf16[32,16,512]{2,1,0:T(8,128)(2,1)} %get-tuple-element.9.a, f32[32,16,256]{2,1,0:T(8,128)} %get-tuple-element.10.b, bf16[128,2048]{1,0:T(8,128)(2,1)} %get-tuple-element.11.c), custom_call_target="tpu_custom_call" | custom-call | tf_op jit(solution)/shard_map/hand_over/pallas_call | solution.py:485

commit v3 on v2

--- a/solution.py
+++ b/solution.py
@@ -233,7 +233,7 @@
     kv_recv = (kv_recv0, kv_recv1)
 
     def peer(i):
-        k = lax.rem(i * jnp.where(side % 2 == 0, 11, 21), POOL)
+        k = lax.rem(i * jnp.where(side % 2 == 0, 5, 27), POOL)
         return lax.rem(row + k // 8, 4) * 8 + lax.rem(col + lax.rem(k, 8), 8)
 
     barrier = pltpu.get_barrier_semaphore()

time: 94.8 us -> 91 us (0.960)
  Pallas kernels: 91.3 us -> 88.3 us
    pallas_call x1, Pallas kernels: 89 us -> 86.1 us  [local(): pl.pallas_call(kernel, out_shape=outs, in_specs=[smem] * 2 + [vmem] * 2 +...]
where the time goes in v3:
time: 91 us; the launch traced here: 90.3 us
  Pallas kernels  88.3 us (97%)
  between operations  1.93 us (2%)
    pallas_call x1, Pallas kernels, local(): pl.pallas_call(kernel, out_shape=outs, in_specs=[smem] * 2 + [vmem] * 2 +...  86.1 us
    pallas_call x1, Pallas kernels, local(): pl.pallas_call(hand_over, out_shape=outs, in_specs=[hbm] * 3, out_specs=(...  2.23 us

profile of v3, /device:TPU:1, one launch (start us, length us, event | category | flops | bytes accessed | tf_op | source)
XLA Modules:
  0.0 90.3 jit_solution(13395798364706532209)
XLA Ops:
  1.9 86.1 %resume.1 = (bf16[32,16,512]{2,1,0:T(8,128)(2,1)}, f32[32,16,256]{2,1,0:T(8,128)}, bf16[128,2048]{1,0:T(8,128)(2,1)}) custom-call(f32[32]{0:T(128)} %rate_s.1, f32[32]{0:T(128)} %gain_s.1, s32[8,128]{1,0:T(8,128)} %bitcast.19, s32[8,128]{1,0:T(8,128)} %bitcast.20, s32[1]{0:T(128)S(6)} %copy.17.hlen_h, s32[1]{0:T(128)S(6)} %copy.18.tlen_h, ...), custom_call_target="tpu_custom_call" | custom-call | tf_op jit(solution)/shard_map/resume/pallas_call | solution.py:435
  88.0 2.2 %hand_over.1 = (bf16[32,16,512]{2,1,0:T(8,128)(2,1)}, f32[32,16,256]{2,1,0:T(8,128)}, bf16[128,2048]{1,0:T(8,128)(2,1)}) custom-call(bf16[32,16,512]{2,1,0:T(8,128)(2,1)} %get-tuple-element.9.a, f32[32,16,256]{2,1,0:T(8,128)} %get-tuple-element.10.b, bf16[128,2048]{1,0:T(8,128)(2,1)} %get-tuple-element.11.c), custom_call_target="tpu_custom_call" | custom-call | tf_op jit(solution)/shard_map/hand_over/pallas_call | solution.py:485
